TPU v7x, 256 devices: a whole 4x4x8 slice. The times are simulated.
256 devices in a mesh: rows: 32 (over z, y_lo, core), chan: 8 (over x, y_hi).
Axes of the slice: x: 4, y: 4 (y_hi: 2, y_lo: 2; y = y_hi * 2 + y_lo), z: 8, core: 2. Of those that a mesh axis runs over, the one named last changes fastest.
Arguments:
- frame_one: bfloat16 [8192, 256], P('rows', 'chan'), may hold values from -6 to 6
- frame_two: bfloat16 [256, 480, 256], P('rows', None, 'chan'), may hold values from -6 to 6
Outputs:
- pyramid: bfloat16 [32, 5040, 8192], P(None, 'chan', 'rows')
All inputs are finite; a program needn't handle non-finite values.
Results may differ from a plain program's by a relative error of at most 0.0016.
Values may be sent and summed in bfloat16 or wider, within the bound.
A program may use at most 128 MiB of HBM per device.

v0:
```python
import jax
import jax.numpy as jnp
from jax import lax
from jax.sharding import PartitionSpec as P


def pool_strip(strip):
    full = strip.astype(jnp.float32)
    rows_n, cols_n, chans = full.shape
    level_one = full.reshape(rows_n // 2, 2, cols_n // 2, 2, chans).mean(axis=(1, 3))
    level_two = level_one.reshape(rows_n // 4, 2, cols_n // 4, 2, chans).mean(axis=(1, 3))
    joined = jnp.concatenate(
        [full.reshape(-1, chans), level_one.reshape(-1, chans), level_two.reshape(-1, chans)],
        axis=0,
    )
    return joined.astype(jnp.bfloat16)


def local(frame_one, frame_two):
    queries = lax.all_gather(frame_one, "chan", axis=1, tiled=True)
    channels = queries.shape[1]
    factor = 1.0 / jnp.sqrt(jnp.float32(channels))
    pooled = pool_strip(frame_two)
    strip_count = lax.axis_size("rows")
    groups = lax.axis_size("chan")
    share = pooled.shape[0] // groups
    slices = pooled.shape[1]
    arranged = jnp.transpose(pooled.reshape(groups, share, slices), (0, 2, 1))
    gathered = lax.all_gather(arranged, "rows", axis=1, tiled=True)
    traded = lax.all_to_all(gathered, "chan", split_axis=0, concat_axis=1, tiled=True)
    traded = traded.reshape(groups, strip_count, slices, share)
    split_queries = queries.reshape(queries.shape[0], groups, slices)
    values = jnp.einsum("kscp,qkc->spq", traded, split_queries, preferred_element_type=jnp.float32)
    return (values * factor).astype(jnp.bfloat16)


def solution(mesh):
    in_specs = (P("rows", "chan"), P("rows", None, "chan"))
    out_specs = P(None, "chan", "rows")
    return jax.shard_map(local, mesh=mesh, in_specs=in_specs, out_specs=out_specs, check_vma=False)
```

profile of v0, /device:TPU:32, one launch (start us, length us, event | category | flops | bytes accessed | tf_op | source)
XLA Modules:
  0.0 323.3 jit_solution(6841564967773849666)
XLA Ops:
  6.5 0.0 all-gather.2.cloned.1.call-start
  6.5 1.1 copy.14
  7.6 1.3 copy.15
  8.9 0.4 reshape.37
  9.3 1.6 reduce_sum.18
  10.9 0.1 broadcast_multiply_fusion
  11.0 0.4 reduce_sum.19
  11.4 0.1 copy.17
  11.5 0.1 copy.22
  11.6 0.1 concatenate.4
  11.7 1.2 convert_element_type.9
  12.9 0.0 all-gather.2.cloned.1.call-update
  12.9 77.1 %all-gather.2.cloned.1.call-done = bf16[8,1024,630]{2,0,1:T(8,128)(2,1)} async-done(((bf16[8,32,630]{2,0,1:T(8,128)(2,1)}), bf16[8,1024,630]{2,0,1:T(8,128)(2,1)}) %all-gather.2.cloned.1.call-update) | async-done | bytes 10321936 | tf_op jit(solution)/shard_map/all_gather | solution.py:29
  90.0 15.1 %copy.18 = bf16[8,1024,630]{1,2,0:T(8,128)(2,1)} copy(bf16[8,1024,630]{2,0,1:T(8,128)(2,1)} %all-gather.2.cloned.1.call-done) | data formatting | bytes 20643840 | tf_op jit(solution)/shard_map/all_gather | solution.py:29
  105.1 0.0 copy-start
  105.1 6.8 %all-to-all-start = ((bf16[8,1024,630]{1,2,0:T(8,128)(2,1)}), bf16[8,1024,630]{1,2,0:T(8,128)(2,1)}, u32[]{:S(2)}, u32[]{:S(2)}) async-start(bf16[8,1024,630]{1,2,0:T(8,128)(2,1)} %copy.18), calls=%async_computation | async-start | bytes 20709376 | tf_op jit(solution)/shard_map/all_to_all | solution.py:30
  112.0 0.0 copy-done
  112.0 168.7 %all_gather.7 = bf16[256,256]{0,1:T(8,128)(2,1)S(1)} all-gather(bf16[256,32]{0,1:T(8,128)(2,1)S(1)} %copy-done), channel_id=1, replica_groups=mesh['rows'=32,'chan'=8] {'chan'}, dimensions={1}, use_global_device_ids=true | all-gather | bytes 147456 | tf_op jit(solution)/shard_map/all_gather | solution.py:20
  280.6 0.0 all-to-all-done
  280.6 14.6 %copy.19 = bf16[8,1024,630]{2,1,0:T(8,128)(2,1)} copy(bf16[8,1024,630]{1,2,0:T(8,128)(2,1)} %all-to-all-done) | data formatting | bytes 20643840 | tf_op jit(solution)/shard_map/all_to_all | solution.py:30
  295.3 10.7 %fusion = bf16[32,630,256]{2,1,0:T(8,128)(2,1)} fusion(bf16[8,32,32,630]{3,2,1,0:T(8,128)(2,1)} %bitcast.21, bf16[256,8,32,1]{0,2,3,1:T(8,128)(2,1)S(1)} %bitcast.27), kind=kOutput, calls=%fused_computation.1 | convolution fusion | flops 2652733440 | bytes 20774912 | tf_op jit(solution)/shard_map/kscp,qkc->spq/dot_general | solution.py:33
  306.0 10.5 %copy.20 = bf16[32,630,256]{2,0,1:T(8,128)(2,1)} copy(bf16[32,630,256]{2,1,0:T(8,128)(2,1)} %fusion) | data formatting | bytes 20643840 | tf_op jit(solution)/shard_map/convert_element_type | solution.py:34
  (1 shorter events, 0.0 us)
Async XLA Ops:
  6.5 83.5 %all-gather.2.cloned.1.call-start = ((), (), s32[]{:S(2)}) async-start(), calls=%async_computation.1 | async-start | bytes 10813440 | tf_op jit(solution)/shard_map/all_gather | solution.py:29
  105.1 6.8 %copy-start = (bf16[256,32]{0,1:T(8,128)(2,1)S(1)}, bf16[256,32]{0,1:T(8,128)(2,1)}, u32[]{:S(2)}) copy-start(bf16[256,32]{0,1:T(8,128)(2,1)} %param.2) | copy-start | bytes 49156
  105.1 175.5 %all-to-all-start = ((bf16[8,1024,630]{1,2,0:T(8,128)(2,1)}), bf16[8,1024,630]{1,2,0:T(8,128)(2,1)}, u32[]{:S(2)}, u32[]{:S(2)}) async-start(bf16[8,1024,630]{1,2,0:T(8,128)(2,1)} %copy.18), calls=%async_computation | async-start | bytes 20709376 | tf_op jit(solution)/shard_map/all_to_all | solution.py:30
Sparse Core Ops, SparseCore 0:
  13.0 76.9 all-gather.1
where the time goes:
time: 324 us; the launch traced here: 323 us
  blocking collectives  169 us (52%)
  waiting for transfers between devices  77.1 us (24%)
  local copies, waits for them, and re-layouts  44.4 us (14%)
  between operations  13.4 us (4%)
  matrix products  10.7 us (3%)
  starting transfers between devices  6.84 us (2%)
    all_gather x1, blocking collectives, local(): queries = lax.all_gather(frame_one, 'chan', axis=1, tiled=True)  169 us
    all_gather x1, waiting for transfers between devices, local(): gathered = lax.all_gather(arranged, 'rows', axis=1, tiled=True)  77.1 us
    all_gather x1, local copies, waits for them, and re-layouts, local(): gathered = lax.all_gather(arranged, 'rows', axis=1, tiled=True)  15.1 us
    all_to_all x1, local copies, waits for them, and re-layouts, local(): lax.all_to_all(gathered, 'chan', split_axis=0, concat_axis=1, tiled=True)  14.6 us
    dot_general x1, matrix products, local(): jnp.einsum('kscp,qkc->spq', traded, split_queries, preferred_element_type...  10.7 us
    convert_element_type x1, local copies, waits for them, and re-layouts, local(): return (values * factor).astype(jnp.bfloat16)  10.5 us
    all_to_all x1, starting transfers between devices, local(): lax.all_to_all(gathered, 'chan', split_axis=0, concat_axis=1, tiled=True)  6.84 us
  transfers between devices with their start and end apart: 2, of which 1 were waited for; matrix products, arithmetic and copies ran while one was open for 0% of the time, Pallas kernels for 0%

commit v1 on v0

--- a/solution.py
+++ b/solution.py
@@ -17,7 +17,9 @@
 
 
 def local(frame_one, frame_two):
-    queries = lax.all_gather(frame_one, "chan", axis=1, tiled=True)
+    queries = jnp.concatenate(
+        lax.all_to_all(jnp.stack([frame_one] * lax.axis_size("chan")), "chan", 0, 0), axis=1
+    )
     channels = queries.shape[1]
     factor = 1.0 / jnp.sqrt(jnp.float32(channels))
     pooled = pool_strip(frame_two)

time: 324 us -> 278 us (0.86)
  blocking collectives: 169 us -> 124 us
  starting transfers between devices: 6.84 us -> 3.37 us
    all_gather x1 -> x0, blocking collectives: 169 us -> none  [local(): queries = lax.all_gather(frame_one, 'chan', axis=1, tiled=True)]
    all_to_all x0 -> x1, blocking collectives: none -> 124 us  [local(): lax.all_to_all(gathered, 'chan', split_axis=0, concat_axis=1, tiled=True)]
    all_to_all x1, starting transfers between devices: 6.84 us -> 3.37 us  [local(): lax.all_to_all(jnp.stack([frame_one] * lax.axis_size('chan')), 'chan', 0, 0)]
  transfers between devices with their start and end apart: 2 -> 2, of which waited for: 1 -> 1; matrix products, arithmetic and copies ran while one was open for 0% -> 5% of each run, Pallas kernels for 0% -> 0%
where the time goes in v1:
time: 278 us; the launch traced here: 276 us
  blocking collectives  124 us (45%)
  waiting for transfers between devices  77.1 us (28%)
  local copies, waits for them, and re-layouts  45.1 us (16%)
  between operations  13.5 us (5%)
  matrix products  10.7 us (4%)
  starting transfers between devices  3.37 us (1%)
    all_to_all x1, blocking collectives, local(): lax.all_to_all(gathered, 'chan', split_axis=0, concat_axis=1, tiled=True)  124 us
    all_gather x1, waiting for transfers between devices, local(): gathered = lax.all_gather(arranged, 'rows', axis=1, tiled=True)  77.1 us
    all_gather x1, local copies, waits for them, and re-layouts, local(): gathered = lax.all_gather(arranged, 'rows', axis=1, tiled=True)  15.1 us
    all_to_all x1, local copies, waits for them, and re-layouts, local(): lax.all_to_all(gathered, 'chan', split_axis=0, concat_axis=1, tiled=True)  14.6 us
    dot_general x1, matrix products, local(): jnp.einsum('kscp,qkc->spq', traded, split_queries, preferred_element_type...  10.7 us
    convert_element_type x1, local copies, waits for them, and re-layouts, local(): return (values * factor).astype(jnp.bfloat16)  10.5 us
  transfers between devices with their start and end apart: 2, of which 1 were waited for; matrix products, arithmetic and copies ran while one was open for 5% of the time, Pallas kernels for 0%

profile of v1, /device:TPU:32, one launch (start us, length us, event | category | flops | bytes accessed | tf_op | source)
XLA Modules:
  0.0 276.0 jit_solution(12364200053475712282)
XLA Ops:
  6.5 0.0 all-gather.2.cloned.1.call-start
  6.5 1.1 copy.14
  7.6 1.3 copy.15
  8.9 0.4 reshape.39
  9.3 1.6 reduce_sum.18
  10.9 0.1 broadcast_multiply_fusion
  11.0 0.4 reduce_sum.19
  11.4 0.1 copy.17
  11.5 0.1 copy.22
  11.6 0.1 concatenate.4
  11.7 1.2 convert_element_type.9
  12.9 0.0 all-gather.2.cloned.1.call-update
  12.9 77.1 %all-gather.2.cloned.1.call-done = bf16[8,1024,630]{2,0,1:T(8,128)(2,1)} async-done(((bf16[8,32,630]{2,0,1:T(8,128)(2,1)}), bf16[8,1024,630]{2,0,1:T(8,128)(2,1)}) %all-gather.2.cloned.1.call-update) | async-done | bytes 10321936 | tf_op jit(solution)/shard_map/all_gather | solution.py:31
  90.0 15.1 %copy.18 = bf16[8,1024,630]{1,2,0:T(8,128)(2,1)} copy(bf16[8,1024,630]{2,0,1:T(8,128)(2,1)} %all-gather.2.cloned.1.call-done) | data formatting | bytes 20643840 | tf_op jit(solution)/shard_map/all_gather | solution.py:31
  105.1 0.0 copy-start
  105.1 124.1 %all_to_all.14 = bf16[8,1024,630]{1,2,0:T(8,128)(2,1)} all-to-all(bf16[8,1024,630]{1,2,0:T(8,128)(2,1)} %copy.18), channel_id=1, replica_groups=mesh['rows'=32,'chan'=8] {'chan'}, dimensions={0} | all-to-all | bytes 20643840 | tf_op jit(solution)/shard_map/all_to_all | solution.py:32
  229.2 0.0 copy-done
  229.2 0.7 stack.2
  229.9 3.4 %all-to-all-start.1 = ((bf16[8,256,32]{1,2,0:T(8,128)(2,1)}), bf16[8,256,32]{1,2,0:T(8,128)(2,1)S(1)}, u32[]{:S(2)}, u32[]{:S(2)}) async-start(bf16[8,256,32]{1,2,0:T(8,128)(2,1)} %stack.2), calls=%async_computation.1 | async-start | bytes 262144 | tf_op jit(solution)/shard_map/all_to_all | solution.py:21
  233.3 14.6 %copy.19 = bf16[8,1024,630]{2,1,0:T(8,128)(2,1)} copy(bf16[8,1024,630]{1,2,0:T(8,128)(2,1)} %all_to_all.14) | data formatting | bytes 20643840 | tf_op jit(solution)/shard_map/all_to_all | solution.py:32
  247.9 0.0 all-to-all-done.1
  247.9 10.7 %fusion = bf16[32,630,256]{2,1,0:T(8,128)(2,1)} fusion(bf16[8,32,32,630]{3,2,1,0:T(8,128)(2,1)} %bitcast.22, bf16[8,256,32]{1,2,0:T(8,128)(2,1)S(1)} %all-to-all-done.1), kind=kOutput, calls=%fused_computation.1 | convolution fusion | flops 2652733440 | bytes 20774912 | tf_op jit(solution)/shard_map/kscp,qkc->spq/dot_general | solution.py:35
  258.6 10.5 %copy.20 = bf16[32,630,256]{2,0,1:T(8,128)(2,1)} copy(bf16[32,630,256]{2,1,0:T(8,128)(2,1)} %fusion) | data formatting | bytes 20643840 | tf_op jit(solution)/shard_map/convert_element_type | solution.py:36
  (1 shorter events, 0.0 us)
Async XLA Ops:
  6.5 83.5 %all-gather.2.cloned.1.call-start = ((), (), s32[]{:S(2)}) async-start(), calls=%async_computation.2 | async-start | bytes 10813440 | tf_op jit(solution)/shard_map/all_gather | solution.py:31
  105.1 124.1 %copy-start = (bf16[256,32]{0,1:T(8,128)(2,1)S(1)}, bf16[256,32]{0,1:T(8,128)(2,1)}, u32[]{:S(2)}) copy-start(bf16[256,32]{0,1:T(8,128)(2,1)} %param.2) | copy-start | bytes 49156
  229.9 18.0 %all-to-all-start.1 = ((bf16[8,256,32]{1,2,0:T(8,128)(2,1)}), bf16[8,256,32]{1,2,0:T(8,128)(2,1)S(1)}, u32[]{:S(2)}, u32[]{:S(2)}) async-start(bf16[8,256,32]{1,2,0:T(8,128)(2,1)} %stack.2), calls=%async_computation.1 | async-start | bytes 262144 | tf_op jit(solution)/shard_map/all_to_all | solution.py:21
Sparse Core Ops, SparseCore 0:
  13.0 76.9 all-gather.1
